TPU v7x, 32 devices: a whole 2x2x4 slice. The times are simulated.
32 devices in a mesh: block: 4 (over y, x), dp: 8 (over z, core).
Axes of the slice: x: 2, y: 2, z: 4, core: 2. Of those that a mesh axis runs over, the one named last changes fastest.
Arguments:
- tokens: bfloat16 [2048, 16384], P('dp', 'block'), may hold values from -6 to 6
- first_up: bfloat16 [128, 128, 128], P('block'), may hold values from -0.5 to 0.5
- second_up: bfloat16 [128, 128, 512], P('block'), may hold values from -0.5 to 0.5
- first_down: bfloat16 [128, 512, 128], P('block'), may hold values from -0.25 to 0.25
- second_down: bfloat16 [128, 128, 128], P('block'), may hold values from -0.5 to 0.5
- cotangent: bfloat16 [2048, 16384], P('dp', 'block'), may hold values from -6 to 6
Outputs:
- output: bfloat16 [2048, 16384], P('dp', 'block')
- input_grad: bfloat16 [2048, 16384], P('dp', 'block')
- grad_first_up: float32 [128, 128, 128], P('block', 'dp')
- grad_second_up: float32 [128, 128, 512], P('block', 'dp')
- grad_first_down: float32 [128, 512, 128], P('block', 'dp')
- grad_second_down: float32 [128, 128, 128], P('block', 'dp')
All inputs are finite; a program needn't handle non-finite values.
Results may differ from a plain program's by a relative error of at most 0.0071.
Values may be sent and summed in bfloat16 or wider, within the bound.
No kernel may reach another device: no remote copies, remote signals or barrier semaphores. Data moves between devices by JAX's collectives and lax.ppermute only.
A program may use at most 192 MiB of HBM per device.

v0:
```python
import math
import jax
import jax.numpy as jnp
from jax import lax
from jax.sharding import PartitionSpec as P


def gelu_pair(values):
    factor = math.sqrt(2.0 / math.pi)
    tanh_part = jnp.tanh(factor * (values + 0.044715 * values * values * values))
    active = 0.5 * values * (1.0 + tanh_part)
    slope_term = 0.5 * (1.0 + tanh_part) + 0.5 * values * (1.0 - tanh_part * tanh_part) * factor * (
        1.0 + 3.0 * 0.044715 * values * values
    )
    return (active, slope_term)


def pack_blocks(array, groups):
    count, local_blocks, width = array.shape
    return (
        array.reshape(count, local_blocks, groups, width // groups)
        .transpose(0, 2, 1, 3)
        .reshape(count, groups, -1)
    )


def unpack_blocks(array, groups, local_blocks):
    count = array.shape[0]
    return (
        array.reshape(count, groups, local_blocks, -1)
        .transpose(0, 2, 1, 3)
        .reshape(count, local_blocks, -1)
    )


def local(tokens, first_up, second_up, first_down, second_down, cotangent):
    narrow = jnp.bfloat16
    wide = jnp.float32
    groups = lax.axis_size("block")
    local_blocks = first_up.shape[0]
    width = first_up.shape[1]
    local_feats = width // groups
    count = tokens.shape[0]
    inputs_b = tokens.reshape(count, local_blocks, width)
    cot_b = cotangent.reshape(count, local_blocks, width)
    mixed_in = jnp.einsum("tbi,bij->tbj", inputs_b, first_up, preferred_element_type=wide).astype(
        narrow
    )
    packed_in = pack_blocks(mixed_in, groups)
    piece = lax.all_to_all(packed_in, "block", split_axis=1, concat_axis=1, tiled=True)
    mixed_piece = piece.reshape(piece.shape[0], -1, local_feats)
    before = jnp.einsum("tbj,jbk->tjk", mixed_piece, second_up, preferred_element_type=wide)
    active, slope_term = gelu_pair(before)
    active_b = active.astype(narrow)
    out_j = jnp.einsum("tjk,jkb->tbj", active_b, first_down, preferred_element_type=wide).astype(
        narrow
    )
    mixed_out = unpack_blocks(
        lax.all_to_all(
            out_j.reshape(count, groups, -1), "block", split_axis=1, concat_axis=1, tiled=True
        ),
        groups,
        local_blocks,
    )
    result = jnp.einsum("tbj,bji->tbi", mixed_out, second_down, preferred_element_type=wide).astype(
        narrow
    )
    g_sd = jnp.einsum("tbj,tbi->bji", mixed_out, cot_b, preferred_element_type=wide)
    back_out = jnp.einsum("tbi,bji->tbj", cot_b, second_down, preferred_element_type=wide).astype(
        narrow
    )
    back_j = lax.all_to_all(
        pack_blocks(back_out, groups), "block", split_axis=1, concat_axis=1, tiled=True
    ).reshape(count, -1, local_feats)
    g_fd = jnp.einsum("tjk,tbj->jkb", active_b, back_j, preferred_element_type=wide)
    back_pre = (
        jnp.einsum("tbj,jkb->tjk", back_j, first_down, preferred_element_type=wide) * slope_term
    ).astype(narrow)
    g_su = jnp.einsum("tbj,tjk->jbk", mixed_piece, back_pre, preferred_element_type=wide)
    back_in_j = jnp.einsum("tjk,jbk->tbj", back_pre, second_up, preferred_element_type=wide).astype(
        narrow
    )
    back_in = unpack_blocks(
        lax.all_to_all(
            back_in_j.reshape(count, groups, -1), "block", split_axis=1, concat_axis=1, tiled=True
        ),
        groups,
        local_blocks,
    )
    g_fu = jnp.einsum("tbi,tbj->bij", inputs_b, back_in, preferred_element_type=wide)
    input_rows = jnp.einsum("tbj,bij->tbi", back_in, first_up, preferred_element_type=wide).astype(
        narrow
    )
    red_fu, red_su, red_fd, red_sd = (
        lax.psum_scatter(g_fu, "dp", scatter_dimension=1, tiled=True),
        lax.psum_scatter(g_su, "dp", scatter_dimension=1, tiled=True),
        lax.psum_scatter(g_fd, "dp", scatter_dimension=1, tiled=True),
        lax.psum_scatter(g_sd, "dp", scatter_dimension=1, tiled=True),
    )
    return (
        result.reshape(count, -1),
        input_rows.reshape(count, -1),
        red_fu,
        red_su,
        red_fd,
        red_sd,
    )


def solution(mesh):
    placed = (
        P("dp", "block"),
        P("block", None, None),
        P("block", None, None),
        P("block", None, None),
        P("block", None, None),
        P("dp", "block"),
    )
    return jax.shard_map(
        local,
        mesh=mesh,
        in_specs=placed,
        out_specs=(
            P("dp", "block"),
            P("dp", "block"),
            P("block", "dp", None),
            P("block", "dp", None),
            P("block", "dp", None),
            P("block", "dp", None),
        ),
        check_vma=False,
    )
```

profile of v0, /device:TPU:0, one launch (start us, length us, event | category | flops | bytes accessed | tf_op | source)
XLA Modules:
  0.0 411.0 jit_solution(18226913873195435735)
XLA Ops:
  7.2 2.8 fusion.18
  11.5 5.3 %all-to-all-start.2 = ((bf16[256,4,1024]{0,2,1:T(8,128)(2,1)}), bf16[256,4,1024]{0,2,1:T(8,128)(2,1)}, u32[]{:S(2)}, u32[]{:S(2)}) async-start(bf16[256,4,1024]{0,2,1:T(8,128)(2,1)} %bitcast.103), calls=%async_computation.2 | async-start | bytes 4194304 | tf_op jit(solution)/shard_map/all_to_all | solution.py:72
  19.1 23.4 %all-to-all-done.2 = bf16[256,4,1024]{0,2,1:T(8,128)(2,1)} async-done(((bf16[256,4,1024]{0,2,1:T(8,128)(2,1)}), bf16[256,4,1024]{0,2,1:T(8,128)(2,1)}, u32[]{:S(2)}, u32[]{:S(2)}) %all-to-all-start.2) | async-done | bytes 2097184 | tf_op jit(solution)/shard_map/all_to_all | solution.py:72
  42.5 4.5 %all-to-all-start = ((bf16[256,4,1024]{0,2,1:T(8,128)(2,1)}), bf16[256,4,1024]{0,2,1:T(8,128)(2,1)}, u32[]{:S(2)}, u32[]{:S(2)}) async-start(bf16[256,4,1024]{0,2,1:T(8,128)(2,1)} %bitcast.102), calls=%async_computation | async-start | bytes 4194304 | tf_op jit(solution)/shard_map/all_to_all | solution.py:50
  47.1 4.5 %copy.60 = bf16[256,128,32]{1,0,2:T(8,128)(2,1)} copy(bf16[256,128,32]{0,2,1:T(8,128)(2,1)} %bitcast.17) | data formatting | bytes 4194304 | tf_op jit(solution)/shard_map/reshape | solution.py:74
  51.6 20.1 %all-to-all-done = bf16[256,4,1024]{0,2,1:T(8,128)(2,1)} async-done(((bf16[256,4,1024]{0,2,1:T(8,128)(2,1)}), bf16[256,4,1024]{0,2,1:T(8,128)(2,1)}, u32[]{:S(2)}, u32[]{:S(2)}) %all-to-all-start) | async-done | bytes 2097184 | tf_op jit(solution)/shard_map/all_to_all | solution.py:50
  71.7 14.1 %multiply_convert_fusion = (bf16[256,32,512]{2,0,1:T(8,128)(2,1)}, f32[32,256,512]{2,1,0:T(8,128)}) fusion(bf16[32,128,512]{2,1,0:T(8,128)(2,1)} %param.8, bf16[256,128,32]{0,2,1:T(8,128)(2,1)} %bitcast.4), kind=kOutput, calls=%fused_computation.10 | convolution fusion | flops 1111490560 | bytes 31457280 | tf_op jit(solution)/shard_map/tbj,jbk->tjk/dot_general | solution.py:52
  85.8 17.3 %fusion.6 = bf16[256,32,512]{2,0,1:T(8,128)(2,1)} fusion(f32[32,256,512]{2,1,0:T(8,128)} %get-tuple-element.25, bf16[256,128,32]{1,0,2:T(8,128)(2,1)S(1)} %copy-done.4, bf16[32,512,128]{2,1,0:T(8,128)(2,1)} %param.9), kind=kOutput, calls=%fused_computation.8 | convolution fusion | flops 1153433600 | bytes 31457280 | tf_op jit(solution)/shard_map/tbj,jkb->tjk/dot_general | solution.py:77
  103.1 6.3 %convert_bitcast_fusion = bf16[256,128,32]{0,1,2:T(8,128)(2,1)S(1)} fusion(bf16[256,32,512]{2,0,1:T(8,128)(2,1)} %fusion.6, bf16[32,128,512]{2,1,0:T(8,128)(2,1)S(1)} %copy-done.5), kind=kOutput, calls=%fused_computation.19 | convolution fusion | flops 1074790400 | bytes 14680064 | tf_op jit(solution)/shard_map/tjk,jbk->tbj/dot_general | solution.py:80
  110.6 27.4 %all_to_all.20 = bf16[256,4,1024]{0,2,1:T(8,128)(2,1)S(1)} all-to-all(bf16[256,4,1024]{0,2,1:T(8,128)(2,1)S(1)} %bitcast.104), channel_id=1, replica_groups=mesh['block'=4,'dp'=8] {'block'}, dimensions={1} | all-to-all | bytes 4194304 | tf_op jit(solution)/shard_map/all_to_all | solution.py:84
  139.5 2.1 fusion.29
  141.6 3.2 copy.65
  144.8 8.8 %convert_bitcast_fusion.1 = bf16[256,128,32]{0,1,2:T(8,128)(2,1)} fusion(bf16[256,32,512]{2,0,1:T(8,128)(2,1)} %get-tuple-element.24, bf16[32,512,128]{2,1,0:T(8,128)(2,1)} %param.9), kind=kOutput, calls=%fused_computation.20 | convolution fusion | flops 1074790400 | bytes 14680064 | tf_op jit(solution)/shard_map/tjk,jkb->tbj/dot_general | solution.py:55
  153.6 2.8 copy.54
  156.4 26.0 %all_to_all.21 = bf16[256,4,1024]{0,2,1:T(8,128)(2,1)S(1)} all-to-all(bf16[256,4,1024]{0,2,1:T(8,128)(2,1)S(1)} %bitcast.106), channel_id=1, replica_groups=mesh['block'=4,'dp'=8] {'block'}, dimensions={1} | all-to-all | bytes 4194304 | tf_op jit(solution)/shard_map/all_to_all | solution.py:59
  184.7 2.0 fusion.7
  186.8 10.2 %fusion.27 = f32[32,128,512]{2,1,0:T(8,128)} fusion(bf16[256,32,512]{2,0,1:T(8,128)(2,1)} %fusion.6, bf16[256,128,32]{0,2,1:T(8,128)(2,1)} %bitcast.4), kind=kOutput, calls=%fused_computation.31 | convolution fusion | flops 1073741824 | bytes 18874368 | tf_op jit(solution)/shard_map/tbj,tjk->jbk/dot_general | solution.py:79
  197.3 9.8 %fusion.32 = f32[32,512,128]{2,1,0:T(8,128)} fusion(bf16[256,32,512]{2,0,1:T(8,128)(2,1)} %get-tuple-element.24, bf16[256,128,32]{1,0,2:T(8,128)(2,1)} %copy.60), kind=kOutput, calls=%fused_computation.34 | convolution fusion | flops 1073741824 | bytes 18874368 | tf_op jit(solution)/shard_map/tjk,tbj->jkb/dot_general | solution.py:75
  207.1 3.6 convolution_convert_fusion
  210.7 4.2 %copy.71 = bf16[256,4096]{1,0:T(8,128)(2,1)} copy(bf16[256,4096]{0,1:T(8,128)(2,1)} %bitcast.108) | data formatting | bytes 4194304
  214.9 3.7 convolution_convert_fusion.1
  218.6 4.1 copy.70
  224.5 89.2 %reduce-scatter.7.cloned.1.call-done = f32[32,16,512]{2,1,0:T(8,128)} async-done(((f32[32,128,512]{2,1,0:T(8,128)}), f32[32,16,512]{2,1,0:T(8,128)}) %reduce-scatter.7.cloned.1.call-update) | async-done | bytes 1048592 | tf_op jit(solution)/shard_map/reduce_scatter | solution.py:96
  313.7 90.7 %reduce-scatter.9.cloned.1.call-done = f32[32,64,128]{2,1,0:T(8,128)} async-done(((f32[32,512,128]{2,1,0:T(8,128)}), f32[32,64,128]{2,1,0:T(8,128)}) %reduce-scatter.9.cloned.1.call-update) | async-done | bytes 1048592 | tf_op jit(solution)/shard_map/reduce_scatter | solution.py:97
  (33 shorter events, 11.2 us)
Async XLA Ops:
  7.2 9.6 %copy-start = (bf16[256,4096]{1,0:T(8,128)(2,1)S(1)}, bf16[256,4096]{1,0:T(8,128)(2,1)}, u32[]{:S(2)}) copy-start(bf16[256,4096]{1,0:T(8,128)(2,1)} %param.6) | copy-start | bytes 6291460
  11.5 5.3 %copy-start.6 = (bf16[32,128,128]{2,1,0:T(8,128)(2,1)S(1)}, bf16[32,128,128]{2,1,0:T(8,128)(2,1)}, u32[]{:S(2)}) copy-start(bf16[32,128,128]{2,1,0:T(8,128)(2,1)} %param.7) | copy-start | bytes 3145732
  11.5 31.1 %all-to-all-start.2 = ((bf16[256,4,1024]{0,2,1:T(8,128)(2,1)}), bf16[256,4,1024]{0,2,1:T(8,128)(2,1)}, u32[]{:S(2)}, u32[]{:S(2)}) async-start(bf16[256,4,1024]{0,2,1:T(8,128)(2,1)} %bitcast.103), calls=%async_computation.2 | async-start | bytes 4194304 | tf_op jit(solution)/shard_map/all_to_all | solution.py:72
  42.5 29.1 %all-to-all-start = ((bf16[256,4,1024]{0,2,1:T(8,128)(2,1)}), bf16[256,4,1024]{0,2,1:T(8,128)(2,1)}, u32[]{:S(2)}, u32[]{:S(2)}) async-start(bf16[256,4,1024]{0,2,1:T(8,128)(2,1)} %bitcast.102), calls=%async_computation | async-start | bytes 4194304 | tf_op jit(solution)/shard_map/all_to_all | solution.py:50
  47.1 175.6 %reduce-scatter.5.cloned.1.call-start = ((), (), s32[]{:S(2)}) async-start(), calls=%async_computation.8 | async-start | bytes 2359296 | tf_op jit(solution)/shard_map/reduce_scatter | solution.py:95
  71.7 14.1 %copy-start.4 = (bf16[256,128,32]{1,0,2:T(8,128)(2,1)S(1)}, bf16[256,128,32]{1,0,2:T(8,128)(2,1)}, u32[]{:S(2)}) copy-start(bf16[256,128,32]{1,0,2:T(8,128)(2,1)} %copy.60) | copy-start | bytes 6291460
  85.8 17.3 %copy-start.5 = (bf16[32,128,512]{2,1,0:T(8,128)(2,1)S(1)}, bf16[32,128,512]{2,1,0:T(8,128)(2,1)}, u32[]{:S(2)}) copy-start(bf16[32,128,512]{2,1,0:T(8,128)(2,1)} %param.8) | copy-start | bytes 12582916
  138.2 1.4 copy-start.1
  144.8 79.7 %reduce-scatter.11.cloned.1.call-start = ((), (), s32[]{:S(2)}) async-start(), calls=%async_computation.11 | async-start | bytes 2359296 | tf_op jit(solution)/shard_map/reduce_scatter | solution.py:98
  182.4 2.3 copy-start.3
  182.6 1.3 copy-start.2
  186.8 126.9 %reduce-scatter.7.cloned.1.call-start = ((), (), s32[]{:S(2)}) async-start(), calls=%async_computation.9 | async-start | bytes 9437184 | tf_op jit(solution)/shard_map/reduce_scatter | solution.py:96
  197.0 207.4 %reduce-scatter.9.cloned.1.call-start = ((), (), s32[]{:S(2)}) async-start(), calls=%async_computation.10 | async-start | bytes 9437184 | tf_op jit(solution)/shard_map/reduce_scatter | solution.py:97
  210.7 4.2 %copy-start.7 = (bf16[32,128,128]{2,1,0:T(8,128)(2,1)S(1)}, bf16[32,128,128]{2,1,0:T(8,128)(2,1)}, u32[]{:S(2)}) copy-start(bf16[32,128,128]{2,1,0:T(8,128)(2,1)} %param.10) | copy-start | bytes 3145732
Sparse Core Ops, SparseCore 0:
  144.9 35.9 reduce-scatter.4
  186.9 35.7 reduce-scatter.10
  225.6 88.0 reduce-scatter.6
  316.4 87.9 reduce-scatter.8
where the time goes:
time: 412 us; the launch traced here: 411 us
  waiting for transfers between devices  224 us (54%)
  matrix products  81.3 us (20%)
  blocking collectives  53.4 us (13%)
  local copies, waits for them, and re-layouts  28.7 us (7%)
  between operations  13.9 us (3%)
  starting transfers between devices  10.2 us (2%)
    reduce_scatter x1, waiting for transfers between devices, local(): lax.psum_scatter(g_fd, 'dp', scatter_dimension=1, tiled=True)  90.7 us
    reduce_scatter x1, waiting for transfers between devices, local(): lax.psum_scatter(g_su, 'dp', scatter_dimension=1, tiled=True)  89.2 us
    all_to_all x1, blocking collectives, local(): lax.all_to_all(back_in_j.reshape(count, groups, -1), 'block', split_axis=...  27.4 us
    all_to_all x1, blocking collectives, local(): lax.all_to_all(out_j.reshape(count, groups, -1), 'block', split_axis=1, c...  26 us
    all_to_all x1, waiting for transfers between devices, local(): lax.all_to_all(pack_blocks(back_out, groups), 'block', split_axis=1, conc...  23.4 us
    all_to_all x1, waiting for transfers between devices, local(): lax.all_to_all(packed_in, 'block', split_axis=1, concat_axis=1, tiled=True)  20.1 us
    dot_general x1, matrix products, local(): jnp.einsum('tbj,jkb->tjk', back_j, first_down, preferred_element_type=wide)  17.3 us
    dot_general x1, matrix products, local(): jnp.einsum('tbj,jbk->tjk', mixed_piece, second_up, preferred_element_type...  14.1 us
  transfers between devices with their start and end apart: 6, of which 4 were waited for; matrix products, arithmetic and copies ran while one was open for 14% of the time, Pallas kernels for 0%

commit v1 on v0

--- a/solution.py
+++ b/solution.py
@@ -47,7 +47,19 @@
         narrow
     )
     packed_in = pack_blocks(mixed_in, groups)
-    piece = lax.all_to_all(packed_in, "block", split_axis=1, concat_axis=1, tiled=True)
+    ways, here = (lax.axis_size("block"), lax.axis_index("block"))
+    width_2 = packed_in.shape[1] // ways
+    dims = list(packed_in.shape)
+    dims[1] = width_2
+    height = dims[1]
+    dims[1] = height * ways
+    full = jnp.zeros(dims, packed_in.dtype)
+    for mask in range(ways):
+        part = lax.dynamic_slice_in_dim(packed_in, (here ^ mask) * width_2, width_2, axis=1)
+        if mask:
+            part = lax.ppermute(part, "block", [(d, d ^ mask) for d in range(ways)])
+        full = lax.dynamic_update_slice_in_dim(full, part, (here ^ mask) * height, axis=1)
+    piece = full
     mixed_piece = piece.reshape(piece.shape[0], -1, local_feats)
     before = jnp.einsum("tbj,jbk->tjk", mixed_piece, second_up, preferred_element_type=wide)
     active, slope_term = gelu_pair(before)

time: 412 us -> 397 us (0.964)
  waiting for transfers between devices: 224 us -> 204 us
  local copies, waits for them, and re-layouts: 28.7 us -> 39.5 us
  blocking collectives: 53.4 us -> 47.7 us
    ppermute x0 -> x3, waiting for transfers between devices: none -> 27.4 us  [local(): part = lax.ppermute(part, 'block', [(d, d ^ mask) for d in range(ways)])]
    all_to_all x1, waiting for transfers between devices: 23.4 us -> 0.01 us  [local(): lax.all_to_all(pack_blocks(back_out, groups), 'block', split_axis=1, conc...]
    all_to_all x1 -> x0, waiting for transfers between devices: 20.1 us -> none  [local(): lax.all_to_all(packed_in, 'block', split_axis=1, concat_axis=1, tiled=True)]
    dynamic_update_slice x0 -> x3, local copies, waits for them, and re-layouts: none -> 5.6 us  [local(): lax.dynamic_update_slice_in_dim(full, part, (here ^ mask) * height, axis=1)]
    all_to_all x1 -> x0, starting transfers between devices: 4.51 us -> none  [local(): lax.all_to_all(packed_in, 'block', split_axis=1, concat_axis=1, tiled=True)]
    ppermute x0 -> x3, starting transfers between devices: none -> 4.48 us  [local(): part = lax.ppermute(part, 'block', [(d, d ^ mask) for d in range(ways)])]
    unnamed x19 -> x21, local copies, waits for them, and re-layouts: 13.5 us -> 16 us
  transfers between devices with their start and end apart: 6 -> 8, of which waited for: 4 -> 4; matrix products, arithmetic and copies ran while one was open for 14% -> 19% of each run, Pallas kernels for 0% -> 0%
where the time goes in v1:
time: 397 us; the launch traced here: 396 us
  waiting for transfers between devices  204 us (51%)
  matrix products  81.1 us (20%)
  blocking collectives  47.7 us (12%)
  local copies, waits for them, and re-layouts  39.5 us (10%)
  between operations  13.9 us (4%)
  starting transfers between devices  9.39 us (2%)
    reduce_scatter x1, waiting for transfers between devices, local(): lax.psum_scatter(g_fd, 'dp', scatter_dimension=1, tiled=True)  90.7 us
    reduce_scatter x1, waiting for transfers between devices, local(): lax.psum_scatter(g_su, 'dp', scatter_dimension=1, tiled=True)  86 us
    ppermute x3, waiting for transfers between devices, local(): part = lax.ppermute(part, 'block', [(d, d ^ mask) for d in range(ways)])  27.4 us
    all_to_all x1, blocking collectives, local(): lax.all_to_all(back_in_j.reshape(count, groups, -1), 'block', split_axis=...  24.8 us
    all_to_all x1, blocking collectives, local(): lax.all_to_all(out_j.reshape(count, groups, -1), 'block', split_axis=1, c...  22.9 us
    dot_general x1, matrix products, local(): jnp.einsum('tbj,jkb->tjk', back_j, first_down, preferred_element_type=wide)  17.6 us
    unnamed x21, local copies, waits for them, and re-layouts  16 us
    dot_general x1, matrix products, local(): jnp.einsum('tbj,jbk->tjk', mixed_piece, second_up, preferred_element_type...  14 us
  transfers between devices with their start and end apart: 8, of which 4 were waited for; matrix products, arithmetic and copies ran while one was open for 19% of the time, Pallas kernels for 0%

profile of v1, /device:TPU:0, one launch (start us, length us, event | category | flops | bytes accessed | tf_op | source)
XLA Modules:
  0.0 395.8 jit_solution(7982508702001988780)
XLA Ops:
  8.8 2.0 fusion.15
  16.0 3.0 collective-permute-start
  22.7 4.5 %all-to-all-start.1 = ((bf16[256,4,1024]{0,2,1:T(8,128)(2,1)}), bf16[256,4,1024]{0,2,1:T(8,128)(2,1)}, u32[]{:S(2)}, u32[]{:S(2)}) async-start(bf16[256,4,1024]{0,2,1:T(8,128)(2,1)} %bitcast.102), calls=%async_computation.1 | async-start | bytes 4194304 | tf_op jit(solution)/shard_map/all_to_all | solution.py:84
  27.3 4.8 %collective-permute-done = bf16[256,1,1024]{0,2,1:T(8,128)(2,1)} collective-permute-done((bf16[256,1,1024]{0,2,1:T(8,128)(2,1)}, bf16[256,1,1024]{0,2,1:T(8,128)(2,1)}, u32[]{:S(2)}, u32[]{:S(2)}) %collective-permute-start) | collective-permute-done | bytes 524320 | tf_op jit(solution)/shard_map/ppermute | solution.py:60
  33.9 22.6 %collective-permute-done.1 = bf16[256,1,1024]{0,2,1:T(8,128)(2,1)} collective-permute-done((bf16[256,1,1024]{0,2,1:T(8,128)(2,1)}, bf16[256,1,1024]{0,2,1:T(8,128)(2,1)}, u32[]{:S(2)}, u32[]{:S(2)}) %collective-permute-start.1) | collective-permute-done | bytes 524320 | tf_op jit(solution)/shard_map/ppermute | solution.py:60
  60.3 14.0 %multiply_convert_fusion = (bf16[256,32,512]{2,0,1:T(8,128)(2,1)}, f32[32,256,512]{2,1,0:T(8,128)}) fusion(bf16[32,128,512]{2,1,0:T(8,128)(2,1)} %param.8, bf16[256,128,32]{0,2,1:T(8,128)(2,1)} %bitcast.5), kind=kOutput, calls=%fused_computation.10 | convolution fusion | flops 1111490560 | bytes 31457280 | tf_op jit(solution)/shard_map/tbj,jbk->tjk/dot_general | solution.py:64
  74.2 4.5 %copy.60 = bf16[256,128,32]{1,0,2:T(8,128)(2,1)} copy(bf16[256,128,32]{0,2,1:T(8,128)(2,1)} %bitcast.18) | data formatting | bytes 4194304 | tf_op jit(solution)/shard_map/reshape | solution.py:86
  78.8 17.6 %fusion.6 = bf16[256,32,512]{2,0,1:T(8,128)(2,1)} fusion(f32[32,256,512]{2,1,0:T(8,128)} %get-tuple-element.29, bf16[256,128,32]{1,0,2:T(8,128)(2,1)} %copy.60, bf16[32,512,128]{2,1,0:T(8,128)(2,1)} %param.9), kind=kOutput, calls=%fused_computation.8 | convolution fusion | flops 1153433600 | bytes 31457280 | tf_op jit(solution)/shard_map/tbj,jkb->tjk/dot_general | solution.py:89
  96.4 6.3 %convert_bitcast_fusion = bf16[256,128,32]{0,1,2:T(8,128)(2,1)S(1)} fusion(bf16[256,32,512]{2,0,1:T(8,128)(2,1)} %fusion.6, bf16[32,128,512]{2,1,0:T(8,128)(2,1)S(1)} %copy-done.6), kind=kOutput, calls=%fused_computation.19 | convolution fusion | flops 1074790400 | bytes 14680064 | tf_op jit(solution)/shard_map/tjk,jbk->tbj/dot_general | solution.py:92
  103.8 24.8 %all_to_all.15 = bf16[256,4,1024]{0,2,1:T(8,128)(2,1)S(1)} all-to-all(bf16[256,4,1024]{0,2,1:T(8,128)(2,1)S(1)} %bitcast.104), channel_id=1, replica_groups=mesh['block'=4,'dp'=8] {'block'}, dimensions={1} | all-to-all | bytes 4194304 | tf_op jit(solution)/shard_map/all_to_all | solution.py:96
  130.2 2.1 fusion.29
  132.3 3.1 copy.65
  135.5 9.0 %convert_bitcast_fusion.1 = bf16[256,128,32]{0,1,2:T(8,128)(2,1)} fusion(bf16[256,32,512]{2,0,1:T(8,128)(2,1)} %get-tuple-element.28, bf16[32,512,128]{2,1,0:T(8,128)(2,1)} %param.9), kind=kOutput, calls=%fused_computation.20 | convolution fusion | flops 1074790400 | bytes 14680064 | tf_op jit(solution)/shard_map/tjk,jkb->tbj/dot_general | solution.py:67
  144.5 2.8 copy.54
  147.3 22.9 %all_to_all.16 = bf16[256,4,1024]{0,2,1:T(8,128)(2,1)S(1)} all-to-all(bf16[256,4,1024]{0,2,1:T(8,128)(2,1)S(1)} %bitcast.106), channel_id=1, replica_groups=mesh['block'=4,'dp'=8] {'block'}, dimensions={1} | all-to-all | bytes 4194304 | tf_op jit(solution)/shard_map/all_to_all | solution.py:71
  172.5 2.1 fusion.7
  174.6 10.4 %fusion.27 = f32[32,128,512]{2,1,0:T(8,128)} fusion(bf16[256,32,512]{2,0,1:T(8,128)(2,1)} %fusion.6, bf16[256,128,32]{0,2,1:T(8,128)(2,1)} %bitcast.5), kind=kOutput, calls=%fused_computation.31 | convolution fusion | flops 1073741824 | bytes 18874368 | tf_op jit(solution)/shard_map/tbj,tjk->jbk/dot_general | solution.py:91
  185.3 9.8 %fusion.32 = f32[32,512,128]{2,1,0:T(8,128)} fusion(bf16[256,32,512]{2,0,1:T(8,128)(2,1)} %get-tuple-element.28, bf16[256,128,32]{1,0,2:T(8,128)(2,1)} %copy.60), kind=kOutput, calls=%fused_computation.41 | convolution fusion | flops 1073741824 | bytes 18874368 | tf_op jit(solution)/shard_map/tjk,tbj->jkb/dot_general | solution.py:87
  195.1 3.7 convolution_convert_fusion.1
  198.8 4.2 %copy.70 = bf16[256,4096]{1,0:T(8,128)(2,1)} copy(bf16[256,4096]{0,1:T(8,128)(2,1)} %bitcast.108) | data formatting | bytes 4194304
  203.0 3.6 convolution_convert_fusion
  206.6 4.1 %copy.71 = bf16[256,4096]{1,0:T(8,128)(2,1)} copy(bf16[256,4096]{0,1:T(8,128)(2,1)} %bitcast.109) | data formatting | bytes 4194304
  212.5 86.0 %reduce-scatter.7.cloned.1.call-done = f32[32,16,512]{2,1,0:T(8,128)} async-done(((f32[32,128,512]{2,1,0:T(8,128)}), f32[32,16,512]{2,1,0:T(8,128)}) %reduce-scatter.7.cloned.1.call-update) | async-done | bytes 1048592 | tf_op jit(solution)/shard_map/reduce_scatter | solution.py:108
  298.5 90.7 %reduce-scatter.9.cloned.1.call-done = f32[32,64,128]{2,1,0:T(8,128)} async-done(((f32[32,512,128]{2,1,0:T(8,128)}), f32[32,64,128]{2,1,0:T(8,128)}) %reduce-scatter.9.cloned.1.call-update) | async-done | bytes 1048592 | tf_op jit(solution)/shard_map/reduce_scatter | solution.py:109
  (44 shorter events, 23.6 us)
Async XLA Ops:
  7.2 1.6 copy-start
  12.3 2.3 copy-start.5
  14.6 5.8 %copy-start.3 = (bf16[256,4096]{1,0:T(8,128)(2,1)S(1)}, bf16[256,4096]{1,0:T(8,128)(2,1)}, u32[]{:S(2)}) copy-start(bf16[256,4096]{1,0:T(8,128)(2,1)} %param.11) | copy-start | bytes 6291460
  14.6 5.8 %copy-start.7 = (bf16[32,128,128]{2,1,0:T(8,128)(2,1)S(1)}, bf16[32,128,128]{2,1,0:T(8,128)(2,1)}, u32[]{:S(2)}) copy-start(bf16[32,128,128]{2,1,0:T(8,128)(2,1)} %param.10) | copy-start | bytes 3145732
  16.0 16.1 %collective-permute-start = (bf16[256,1,1024]{0,2,1:T(8,128)(2,1)}, bf16[256,1,1024]{0,2,1:T(8,128)(2,1)}, u32[]{:S(2)}, u32[]{:S(2)}) collective-permute-start(bf16[256,1,1024]{0,2,1:T(8,128)(2,1)} %get-tuple-element.26), channel_id=1, source_target_pairs={{0,8},{8,0},{16,24},{24,16},{1,9},{9,1},{17,25},{25,17},{2,10},{10... | collective-permute-start | bytes 1572872 | tf_op jit(solution)/shard_map/ppermute | solution.py:60
  19.0 37.6 %collective-permute-start.1 = (bf16[256,1,1024]{0,2,1:T(8,128)(2,1)}, bf16[256,1,1024]{0,2,1:T(8,128)(2,1)}, u32[]{:S(2)}, u32[]{:S(2)}) collective-permute-start(bf16[256,1,1024]{0,2,1:T(8,128)(2,1)} %get-tuple-element.25), channel_id=1, source_target_pairs={{0,16},{8,24},{16,0},{24,8},{1,17},{9,25},{17,1},{25,9},{2,18},{10... | collective-permute-start | bytes 1572872 | tf_op jit(solution)/shard_map/ppermute | solution.py:60
  20.5 37.9 %collective-permute-start.2 = (bf16[256,1,1024]{0,2,1:T(8,128)(2,1)}, bf16[256,1,1024]{0,2,1:T(8,128)(2,1)}, u32[]{:S(2)}, u32[]{:S(2)}) collective-permute-start(bf16[256,1,1024]{0,2,1:T(8,128)(2,1)} %get-tuple-element.24), channel_id=1, source_target_pairs={{0,24},{8,16},{16,8},{24,0},{1,25},{9,17},{17,9},{25,1},{2,26},{10... | collective-permute-start | bytes 1572872 | tf_op jit(solution)/shard_map/ppermute | solution.py:60
  22.7 51.5 %all-to-all-start.1 = ((bf16[256,4,1024]{0,2,1:T(8,128)(2,1)}), bf16[256,4,1024]{0,2,1:T(8,128)(2,1)}, u32[]{:S(2)}, u32[]{:S(2)}) async-start(bf16[256,4,1024]{0,2,1:T(8,128)(2,1)} %bitcast.102), calls=%async_computation.1 | async-start | bytes 4194304 | tf_op jit(solution)/shard_map/all_to_all | solution.py:84
  27.2 183.4 %reduce-scatter.5.cloned.1.call-start = ((), (), s32[]{:S(2)}) async-start(), calls=%async_computation.7 | async-start | bytes 2359296 | tf_op jit(solution)/shard_map/reduce_scatter | solution.py:107
  78.8 17.6 %copy-start.6 = (bf16[32,128,512]{2,1,0:T(8,128)(2,1)S(1)}, bf16[32,128,512]{2,1,0:T(8,128)(2,1)}, u32[]{:S(2)}) copy-start(bf16[32,128,512]{2,1,0:T(8,128)(2,1)} %param.8) | copy-start | bytes 12582916
  128.9 1.4 copy-start.1
  135.4 77.1 %reduce-scatter.11.cloned.1.call-start = ((), (), s32[]{:S(2)}) async-start(), calls=%async_computation.10 | async-start | bytes 2359296 | tf_op jit(solution)/shard_map/reduce_scatter | solution.py:110
  170.1 2.3 copy-start.4
  170.4 1.3 copy-start.2
  174.6 123.9 %reduce-scatter.7.cloned.1.call-start = ((), (), s32[]{:S(2)}) async-start(), calls=%async_computation.8 | async-start | bytes 9437184 | tf_op jit(solution)/shard_map/reduce_scatter | solution.py:108
  185.0 204.2 %reduce-scatter.9.cloned.1.call-start = ((), (), s32[]{:S(2)}) async-start(), calls=%async_computation.9 | async-start | bytes 9437184 | tf_op jit(solution)/shard_map/reduce_scatter | solution.py:109
  198.8 4.2 %copy-start.8 = (bf16[32,128,128]{2,1,0:T(8,128)(2,1)S(1)}, bf16[32,128,128]{2,1,0:T(8,128)(2,1)}, u32[]{:S(2)}) copy-start(bf16[32,128,128]{2,1,0:T(8,128)(2,1)} %param.7) | copy-start | bytes 3145732
Sparse Core Ops, SparseCore 0:
  135.5 32.7 reduce-scatter.4
  174.7 32.5 reduce-scatter.10
  210.2 88.2 reduce-scatter.6
  301.2 87.9 reduce-scatter.8
